TPU v7x, 256 devices: a whole 4x4x8 slice. The times are simulated.
256 devices in a mesh: row: 32 (over x, y, core), col: 8 (over z).
Axes of the slice: x: 4, y: 4, z: 8, core: 2. Of those that a mesh axis runs over, the one named last changes fastest.
Arguments:
- matrix: float32 [65536, 5, 8, 128], P('row', None, 'col'), may hold values from -320 to 320, as said below
Outputs:
- r_rows: float32 [256, 5, 8, 128], P(None, None, 'col')
- residual: float32 [65536, 5, 8, 128], P('row', None, 'col')
Inputs may be any that keep to these rules, and one draw needn't show every extreme that they name: `matrix`: real entries; the first 256 columns have full column rank on every block of 2048 rows.
All inputs are finite; a program needn't handle non-finite values.
Results may differ from a plain program's by a relative error of at most 0.0003.
Values sent between devices are 32-bit elements; how exact they have to be, the bound alone decides.
No kernel may reach another device: no remote copies, remote signals or barrier semaphores. Data moves between devices by JAX's collectives and lax.ppermute only.
A program may use at most 128 MiB of HBM per device.

v0:
```python
import math
import jax
import jax.numpy as jnp
from jax import lax
from jax.sharding import PartitionSpec as P


def broadcast(value, axis, root):
    mine = lax.axis_index(axis) == root
    return lax.psum(jnp.where(mine, value, jnp.zeros_like(value)), axis)


def cross_product(left, right):
    return jnp.einsum(
        "mk,mn->kn",
        left,
        right,
        precision=lax.Precision.HIGHEST,
        preferred_element_type=jnp.float32,
    )


def matmul(left, right):
    return jnp.dot(left, right, precision=lax.Precision.HIGHEST, preferred_element_type=jnp.float32)


def factor_pair(gram):
    size = gram.shape[0]
    if size == 1:
        root = jnp.sqrt(gram)
        return (root, 1.0 / root)
    half = size // 2
    first_up, first_inv = factor_pair(gram[:half, :half])
    coupling = cross_product(first_inv, gram[:half, half:])
    schur = gram[half:, half:] - cross_product(coupling, coupling)
    second_up, second_inv = factor_pair(schur)
    lower_zero = jnp.zeros((size - half, half), jnp.float32)
    upper = jnp.concatenate(
        [
            jnp.concatenate([first_up, coupling], axis=1),
            jnp.concatenate([lower_zero, second_up], axis=1),
        ],
        axis=0,
    )
    corner = -matmul(matmul(first_inv, coupling), second_inv)
    inverse = jnp.concatenate(
        [
            jnp.concatenate([first_inv, corner], axis=1),
            jnp.concatenate([lower_zero, second_inv], axis=1),
        ],
        axis=0,
    )
    return (upper, inverse)


def project_after(inverse, panel, local, summed):
    basis_rows = matmul(panel, inverse)
    top = summed(cross_product(basis_rows, local))
    residual = local - matmul(basis_rows, top)
    return (top, residual)


def per_device(matrix):
    rows_here = matrix.shape[0]
    blocks = matrix.shape[1]
    width = matrix.shape[3]
    local = matrix.reshape(rows_here, blocks * width)
    pieces = []
    for owner in range(2):
        pieces.append(broadcast(matrix[:, 0, 0, :], "col", owner))
    panel = jnp.concatenate(pieces, axis=1)
    total_rows = rows_here * lax.axis_size("row")
    gram = cross_product(panel, panel)
    upper, inverse = factor_pair(lax.psum(gram, "row"))

    def summed(value):
        return lax.psum(value, "row")

    top, residual = project_after(inverse, panel, local, summed)
    scaled = top / math.sqrt(total_rows)
    return (
        scaled.reshape(top.shape[0], blocks, 1, width),
        residual.reshape(rows_here, blocks, 1, width),
    )


def solution(mesh):
    return jax.shard_map(
        per_device,
        mesh=mesh,
        in_specs=(P("row", None, "col", None),),
        out_specs=(P(None, None, "col", None), P("row", None, "col", None)),
        check_vma=False,
    )
```

profile of v0, /device:TPU:1, one launch (start us, length us, event | category | flops | bytes accessed | tf_op | source)
XLA Modules:
  0.0 833.4 jit_solution(13384232351015259897)
XLA Ops:
  7.3 3.3 broadcast_select_fusion
  10.6 1.0 select_bitcast_fusion
  11.7 82.9 %all-reduce.136.cloned.1.call-done = (f32[2048,128]{1,0:T(8,128)}, f32[2048,128]{1,0:T(8,128)}) async-done(((f32[2048,128]{1,0:T(8,128)}, f32[2048,128]{1,0:T(8,128)}), (f32[2048,128]{1,0:T(8,128)}, f32[2048,128]{1,0:T(8,128)})) %all-reduce.136.cloned.1.call-update) | async-done | bytes 2097168 | tf_op jit(solution)/shard_map/psum | solution.py:10
  94.6 1.4 constant_dynamic-update-slice_fusion.1
  96.2 4.2 fusion.1342
  100.5 12.0 %copy.264 = f32[2048,5,1,128]{0,3,1,2:T(8,128)} copy(f32[2048,5,1,128]{3,2,1,0:T(1,128)} %param.1) | data formatting | bytes 10485760 | tf_op args[0]
  112.5 101.5 %all-reduce.132.cloned.1.call-done = f32[256,256]{1,0:T(8,128)} async-done(((f32[256,256]{1,0:T(8,128)}), f32[256,256]{1,0:T(8,128)}) %all-reduce.132.cloned.1.call-update) | async-done | bytes 262160 | tf_op jit(solution)/shard_map/psum | solution.py:74
  214.0 1.5 fusion.1214
  217.5 0.9 fusion.928
  218.6 0.9 convolution_subtract_fusion.127
  222.2 1.0 fusion.735
  223.4 0.9 convolution_subtract_fusion.63
  230.6 1.0 fusion.511
  231.8 0.9 convolution_subtract_fusion.31
  246.2 1.0 fusion.319
  247.4 0.9 convolution_subtract_fusion.15
  265.7 0.7 fusion.1335
  276.4 1.0 fusion.191
  277.6 0.9 convolution_subtract_fusion.7
  295.9 0.7 fusion.1331
  310.4 0.7 fusion.1329
  324.6 0.7 fusion.1327
  331.8 0.7 fusion.1326
  353.4 0.7 fusion.1323
  367.4 0.7 fusion.1321
  381.3 0.7 fusion.1319
  395.4 0.7 fusion.1317
  409.3 0.7 fusion.1315
  423.4 0.7 fusion.1313
  465.9 0.7 fusion.1307
  479.9 0.7 fusion.1305
  493.8 0.7 fusion.1303
  508.0 0.7 fusion.1301
  521.8 0.7 fusion.1299
  535.9 0.7 fusion.1297
  564.2 0.7 fusion.1293
  578.0 0.7 fusion.1291
  592.1 0.7 fusion.1289
  620.2 0.7 fusion.1285
  673.2 2.0 fusion
  675.2 1.3 copy-done
  676.4 13.2 %fusion.1408 = f32[256,640]{1,0:T(8,128)} fusion(f32[2048,256]{1,0:T(8,128)S(1)} %fusion, f32[2048,640]{0,1:T(8,128)} %bitcast.1420), kind=kOutput, calls=%fused_computation.1806 | convolution fusion | flops 4026531840 | bytes 7995392 | tf_op jit(solution)/shard_map/mk,mn->kn/dot_general | solution.py:14
  689.6 113.0 %all-reduce.134.cloned.1.call-done = f32[256,640]{1,0:T(8,128)} async-done(((f32[256,640]{1,0:T(8,128)}), f32[256,640]{1,0:T(8,128)}) %all-reduce.134.cloned.1.call-update) | async-done | bytes 655376 | tf_op jit(solution)/shard_map/psum | solution.py:77
  802.6 2.0 broadcast_multiply_fusion
  804.7 1.3 copy.265
  806.0 1.1 copy.266
  807.2 7.9 convolution_subtract_fusion
  815.1 11.5 %copy.267 = f32[2048,5,1,128]{3,2,1,0:T(1,128)} copy(f32[2048,5,1,128]{0,3,1,2:T(8,128)} %bitcast.1422) | data formatting | bytes 10485760
  (876 shorter events, 184.5 us)
Async XLA Ops:
  7.2 87.4 %all-reduce.136.cloned.1.call-start = ((), (), s32[]{:S(2)}) async-start(), calls=%async_computation.2 | async-start | bytes 4194304 | tf_op jit(solution)/shard_map/psum | solution.py:10
  11.6 202.3 %all-reduce.132.cloned.1.call-start = ((), (), s32[]{:S(2)}) async-start(), calls=%async_computation | async-start | bytes 524288 | tf_op jit(solution)/shard_map/psum | solution.py:74
  94.6 1.5 copy-start.3
  100.4 702.2 %all-reduce.134.cloned.1.call-start = ((), (), s32[]{:S(2)}) async-start(), calls=%async_computation.1 | async-start | bytes 1310720 | tf_op jit(solution)/shard_map/psum | solution.py:77
  214.0 121.7 %copy-start.4 = (f32[256,256]{1,0:T(8,128)S(1)}, f32[256,256]{1,0:T(8,128)}, u32[]{:S(2)}) copy-start(f32[256,256]{1,0:T(8,128)} %all-reduce.132.cloned.1.call-done) | copy-start | bytes 786436
  675.1 1.3 copy-start
  689.6 117.5 %copy-start.1 = (f32[2048,256]{1,0:T(8,128)S(1)}, f32[2048,256]{1,0:T(8,128)}, u32[]{:S(2)}) copy-start(f32[2048,256]{1,0:T(8,128)} %copy-done) | copy-start | bytes 6291460
  802.6 4.5 copy-start.2
Sparse Core Ops, SparseCore 0:
  11.8 82.7 all-reduce.135
  100.5 113.4 all-reduce.131
  689.7 112.8 all-reduce.133
where the time goes:
time: 842 us; the launch traced here: 833 us
  waiting for transfers between devices  297 us (35%)
  between operations  264 us (31%)
  matrix products  130 us (15%)
  local copies, waits for them, and re-layouts  120 us (14%)
  other arithmetic  22 us (3%)
    psum x1, waiting for transfers between devices, summed(): return lax.psum(value, 'row')  113 us
    psum x1, waiting for transfers between devices, per_device(): upper, inverse = factor_pair(lax.psum(gram, 'row'))  102 us
    slice x128, local copies, waits for them, and re-layouts, factor_pair(): coupling = cross_product(first_inv, gram[:half, half:])  86.2 us
    psum x1, waiting for transfers between devices, broadcast(): return lax.psum(jnp.where(mine, value, jnp.zeros_like(value)), axis)  82.9 us
    dot_general x256, matrix products, cross_product(): jnp.einsum('mk,mn->kn', left, right, precision=lax.Precision.HIGHEST, pre...  79.4 us
    dot_general x256, matrix products, matmul(): jnp.dot(left, right, precision=lax.Precision.HIGHEST, preferred_element_t...  50.2 us
    unnamed x14, local copies, waits for them, and re-layouts  27.5 us
  transfers between devices with their start and end apart: 3, of which 3 were waited for; matrix products, arithmetic and copies ran while one was open for 1% of the time, Pallas kernels for 0%

commit v1 on v0

--- a/solution.py
+++ b/solution.py
@@ -3,11 +3,17 @@
 import jax.numpy as jnp
 from jax import lax
 from jax.sharding import PartitionSpec as P
+from jax.lax import all_gather
+
+
+def remake_trees(u, which_axis):
+    x_new = all_gather(u, axis_name=which_axis)
+    return jnp.sum(x_new, axis=0)
 
 
 def broadcast(value, axis, root):
     mine = lax.axis_index(axis) == root
-    return lax.psum(jnp.where(mine, value, jnp.zeros_like(value)), axis)
+    return remake_trees(jnp.where(mine, value, jnp.zeros_like(value)), axis)
 
 
 def cross_product(left, right):

time: 842 us -> 948 us (1.13)
  waiting for transfers between devices: 297 us -> 400 us
    all_gather x0 -> x2, waiting for transfers between devices: none -> 188 us  [remake_trees(): x_new = all_gather(u, axis_name=which_axis)]
    psum x1 -> x0, waiting for transfers between devices: 82.9 us -> none  [broadcast(): return lax.psum(jnp.where(mine, value, jnp.zeros_like(value)), axis)]
    unnamed x14 -> x9, local copies, waits for them, and re-layouts: 27.5 us -> 24.7 us
  transfers between devices with their start and end apart: 3 -> 4, of which waited for: 3 -> 4; matrix products, arithmetic and copies ran while one was open for 1% -> 2% of each run, Pallas kernels for 0% -> 0%
where the time goes in v1:
time: 948 us; the launch traced here: 939 us
  waiting for transfers between devices  400 us (42%)
  between operations  263 us (28%)
  matrix products  130 us (14%)
  local copies, waits for them, and re-layouts  117 us (12%)
  other arithmetic  29 us (3%)
    all_gather x2, waiting for transfers between devices, remake_trees(): x_new = all_gather(u, axis_name=which_axis)  188 us
    psum x1, waiting for transfers between devices, summed(): return lax.psum(value, 'row')  113 us
    psum x1, waiting for transfers between devices, per_device(): upper, inverse = factor_pair(lax.psum(gram, 'row'))  98 us
    slice x128, local copies, waits for them, and re-layouts, factor_pair(): coupling = cross_product(first_inv, gram[:half, half:])  86 us
    dot_general x256, matrix products, cross_product(): jnp.einsum('mk,mn->kn', left, right, precision=lax.Precision.HIGHEST, pre...  78.9 us
    dot_general x256, matrix products, matmul(): jnp.dot(left, right, precision=lax.Precision.HIGHEST, preferred_element_t...  51.4 us
    unnamed x9, local copies, waits for them, and re-layouts  24.7 us
  transfers between devices with their start and end apart: 4, of which 4 were waited for; matrix products, arithmetic and copies ran while one was open for 2% of the time, Pallas kernels for 0%

profile of v1, /device:TPU:1, one launch (start us, length us, event | category | flops | bytes accessed | tf_op | source)
XLA Modules:
  0.0 939.2 jit_solution(10216093612583078460)
XLA Ops:
  7.2 3.5 broadcast_select_fusion.1
  10.8 0.7 all-gather.7.cloned.1.call-update
  11.5 97.3 %all-gather.5.cloned.1.call-done = f32[16384,1,1,128]{3,2,1,0:T(1,128)} async-done(((f32[2048,1,1,128]{3,2,1,0:T(1,128)}), f32[16384,1,1,128]{3,2,1,0:T(1,128)}) %all-gather.5.cloned.1.call-update) | async-done | bytes 8388624 | tf_op jit(solution)/shard_map/all_gather | solution.py:10
  108.8 3.9 reduce_sum.18
  112.7 90.7 %all-gather.7.cloned.1.call-done = f32[16384,1,1,128]{3,2,1,0:T(1,128)} async-done(((f32[2048,1,1,128]{3,2,1,0:T(1,128)}), f32[16384,1,1,128]{3,2,1,0:T(1,128)}) %all-gather.7.cloned.1.call-update) | async-done | bytes 8388624 | tf_op jit(solution)/shard_map/all_gather | solution.py:10
  203.4 3.9 reduce_sum.19
  207.3 4.2 fusion.1
  211.6 12.0 %copy.392 = f32[2048,5,1,128]{0,3,1,2:T(8,128)} copy(f32[2048,5,1,128]{3,2,1,0:T(1,128)} %param.1) | data formatting | bytes 10485760 | tf_op args[0]
  223.6 98.0 %all-reduce.130.cloned.1.call-done = f32[256,256]{1,0:T(8,128)} async-done(((f32[256,256]{1,0:T(8,128)}), f32[256,256]{1,0:T(8,128)}) %all-reduce.130.cloned.1.call-update) | async-done | bytes 262160 | tf_op jit(solution)/shard_map/psum | solution.py:80
  321.6 1.5 fusion.1216
  325.1 0.8 fusion.928
  326.1 0.9 convolution_subtract_fusion.127
  329.6 0.9 fusion.736
  330.8 0.9 convolution_subtract_fusion.63
  337.7 0.9 fusion.512
  338.9 0.9 convolution_subtract_fusion.31
  349.6 0.7 fusion.1340
  352.9 1.0 fusion.320
  354.1 0.9 convolution_subtract_fusion.15
  364.8 0.7 fusion.1338
  371.8 0.7 fusion.1337
  382.3 1.0 fusion.192
  383.5 0.9 convolution_subtract_fusion.7
  401.3 0.7 fusion.1333
  415.4 0.7 fusion.1331
  429.3 0.7 fusion.1329
  486.0 0.7 fusion.1321
  514.3 0.7 fusion.1317
  528.5 0.7 fusion.1315
  542.5 0.7 fusion.1313
  599.3 0.7 fusion.1305
  627.7 0.7 fusion.1301
  641.8 0.7 fusion.1299
  655.8 0.7 fusion.1297
  684.3 0.7 fusion.1293
  698.5 0.7 fusion.1291
  712.5 0.7 fusion.1289
  726.8 0.7 fusion.1287
  740.7 0.7 fusion.1285
  754.8 0.7 fusion.1283
  779.5 3.1 fusion
  782.7 12.8 %fusion.1409 = f32[256,640]{1,0:T(8,128)} fusion(f32[2048,256]{1,0:T(8,128)S(1)} %fusion, f32[2048,640]{0,1:T(8,128)} %bitcast.1414), kind=kOutput, calls=%fused_computation.1806 | convolution fusion | flops 4026531840 | bytes 7995392 | tf_op jit(solution)/shard_map/mk,mn->kn/dot_general | solution.py:20
  795.5 113.0 %all-reduce.132.cloned.1.call-done = f32[256,640]{1,0:T(8,128)} async-done(((f32[256,640]{1,0:T(8,128)}), f32[256,640]{1,0:T(8,128)}) %all-reduce.132.cloned.1.call-update) | async-done | bytes 655376 | tf_op jit(solution)/shard_map/psum | solution.py:83
  908.5 2.0 broadcast_multiply_fusion
  910.5 1.3 copy.393
  911.8 1.1 copy.394
  913.0 7.9 convolution_subtract_fusion
  920.9 11.5 %copy.395 = f32[2048,5,1,128]{3,2,1,0:T(1,128)} copy(f32[2048,5,1,128]{0,3,1,2:T(8,128)} %bitcast.1416) | data formatting | bytes 10485760
  (873 shorter events, 184.7 us)
Async XLA Ops:
  7.2 101.7 %all-gather.5.cloned.1.call-start = ((), (), s32[]{:S(2)}) async-start(), calls=%async_computation.2 | async-start | bytes 9437184 | tf_op jit(solution)/shard_map/all_gather | solution.py:10
  10.7 192.7 %all-gather.7.cloned.1.call-start = ((), (), s32[]{:S(2)}) async-start(), calls=%async_computation.3 | async-start | bytes 9437184 | tf_op jit(solution)/shard_map/all_gather | solution.py:10
  11.5 310.1 %all-reduce.130.cloned.1.call-start = ((), (), s32[]{:S(2)}) async-start(), calls=%async_computation | async-start | bytes 524288 | tf_op jit(solution)/shard_map/psum | solution.py:80
  207.3 16.3 %copy-start = (f32[2048,128]{1,0:T(8,128)}, f32[2048,128]{1,0:T(8,128)S(1)}, u32[]{:S(2)}) copy-start(f32[2048,128]{1,0:T(8,128)S(1)} %reduce_sum.19) | copy-start | bytes 3145732
  211.5 697.0 %all-reduce.132.cloned.1.call-start = ((), (), s32[]{:S(2)}) async-start(), calls=%async_computation.1 | async-start | bytes 1310720 | tf_op jit(solution)/shard_map/psum | solution.py:83
  321.6 118.6 %copy-start.2 = (f32[256,256]{1,0:T(8,128)S(1)}, f32[256,256]{1,0:T(8,128)}, u32[]{:S(2)}) copy-start(f32[256,256]{1,0:T(8,128)} %all-reduce.130.cloned.1.call-done) | copy-start | bytes 786436
  908.5 4.5 copy-start.1
Sparse Core Ops, SparseCore 0:
  10.9 97.9 all-gather.4
  110.6 92.7 all-gather.6
  211.6 109.8 all-reduce.129
  795.6 112.8 all-reduce.131
